TPU v7x, 32 devices: a whole 2x2x4 slice. The times are simulated.
32 devices in a mesh: groups: 2 (over y), vocab: 8 (over z, x), mp: 2 (over core).
Axes of the slice: x: 2, y: 2, z: 4, core: 2. Of those that a mesh axis runs over, the one named last changes fastest.
Arguments:
- gate_pre: bfloat16 [32, 14336], P(('groups', 'vocab'), 'mp'), parts along dimension 0, may hold values from -6 to 6
- up_pre: bfloat16 [32, 14336], P(('groups', 'vocab'), 'mp'), parts along dimension 0, may hold values from -6 to 6
- down_weight: bfloat16 [8192, 14336], P('vocab', 'mp'), may hold values from -0.046875 to 0.046875
- residual: bfloat16 [32, 8192], P(('groups', 'vocab', 'mp')), parts along dimension 0, may hold values from -36 to 36
- norm_gain: bfloat16 [8192], replicated, may hold values from 0.5 to 1.5
- head_weight: bfloat16 [8192, 4032], P('mp', 'vocab')
- targets: int32 [32], P(('groups', 'mp')), parts along dimension 0, may hold values from 0 to 4031
Outputs:
- log_likelihood: float32 [32], P(('groups', 'mp')), parts along dimension 0
There are 2 independent parts, one for each index of `groups`. A program takes and returns all parts, laid end to end along the dimension named above; an argument that names none is the same for every part. Nothing has to cross between parts.
All inputs are finite; a program needn't handle non-finite values.
Results may differ from a plain program's by a relative error of at most 0.0003.
The roundings to bfloat16 on the way count: a program that leaves them out, or rounds other values in their place, can miss the bound.
Values may be sent and summed in bfloat16 or wider, within the bound.
No kernel may reach another device: no remote copies, remote signals or barrier semaphores. Data moves between devices by JAX's collectives and lax.ppermute only.
A program may use at most 64 MiB of HBM per device.

v0:
```python
import jax
import jax.numpy as jnp
from jax import lax
from jax.sharding import PartitionSpec as P

EPSILON = 1e-05


def merged_2(value, axis, combine):
    everything = jax.tree.map(lambda part: lax.all_gather(part, axis), value)
    first = jax.tree.map(lambda part: part[0], everything)

    def turn(k, so_far):
        return combine(so_far, jax.tree.map(lambda part: part[k], everything))

    return lax.fori_loop(1, lax.axis_size(axis), turn, first)


def merge_stats(earlier, follows):
    joint_max = jnp.maximum(earlier[0], follows[0])
    joint_sum = earlier[1] * jnp.exp(earlier[0] - joint_max) + follows[1] * jnp.exp(
        follows[0] - joint_max
    )
    return (joint_max, joint_sum, earlier[2] + follows[2])


def body(gate_pre, up_pre, down_weight, residual, norm_gain, head_weight, targets):
    vocab_count = lax.axis_size("vocab")
    model_count = lax.axis_size("mp")
    model_index = lax.axis_index("mp")
    vocab_index = lax.axis_index("vocab")
    gated_units = (jax.nn.silu(gate_pre.astype(jnp.float32)) * up_pre.astype(jnp.float32)).astype(
        jnp.bfloat16
    )
    down_terms = lax.dot_general(
        lax.all_gather(gated_units, "vocab", axis=0, tiled=True),
        down_weight,
        (((1,), (1,)), ((), ())),
        preferred_element_type=jnp.float32,
    )
    own_rows = residual.shape[0]
    block_cols = down_weight.shape[0]
    grouped = down_terms.reshape(vocab_count, model_count, own_rows, block_cols)
    arrived = lax.all_to_all(
        lax.all_to_all(grouped, "vocab", split_axis=0, concat_axis=3, tiled=True),
        "mp",
        split_axis=1,
        concat_axis=0,
        tiled=True,
    )
    update = jnp.sum(arrived, axis=(0, 1))
    stream = (residual.astype(jnp.float32) + update).astype(jnp.bfloat16)
    stream = lax.optimization_barrier(stream)
    widened = stream.astype(jnp.float32)
    mean_square = jnp.mean(widened * widened, axis=1, keepdims=True)
    normed = (
        widened * lax.rsqrt(mean_square + EPSILON) * norm_gain.astype(jnp.float32)[None, :]
    ).astype(jnp.bfloat16)
    half_width = head_weight.shape[0]
    halves = lax.dynamic_slice_in_dim(
        lax.all_gather(normed, ("vocab", "mp"), axis=0, tiled=True),
        model_index * half_width,
        half_width,
        1,
    )
    logit_terms = jnp.dot(halves, head_weight, preferred_element_type=jnp.float32)
    logits = lax.psum_scatter(logit_terms, "mp", scatter_dimension=0, tiled=True)
    local_ids = targets - vocab_index * logits.shape[1]
    columns = lax.broadcasted_iota(jnp.int32, logits.shape, 1)
    chosen = jnp.sum(jnp.where(columns == local_ids[:, None], logits, 0.0), axis=1)
    row_top = jnp.max(logits, axis=1)
    exp_total = jnp.sum(jnp.exp(logits - row_top[:, None]), axis=1)
    merged = merged_2((row_top, exp_total, chosen), "vocab", merge_stats)
    return merged[2] - merged[0] - jnp.log(merged[1])


def solution(mesh):
    return jax.shard_map(
        body,
        mesh=mesh,
        in_specs=(
            P(("groups", "vocab"), "mp"),
            P(("groups", "vocab"), "mp"),
            P("vocab", "mp"),
            P(("groups", "vocab", "mp"), None),
            P(),
            P("mp", "vocab"),
            P(("groups", "mp")),
        ),
        out_specs=P(("groups", "mp")),
        check_vma=False,
    )
```

profile of v0, /device:TPU:0, one launch (start us, length us, event | category | flops | bytes accessed | tf_op | source)
XLA Modules:
  0.0 128.8 jit_solution(11626139243467973319)
XLA Ops:
  6.5 0.0 copy-start.3
  6.5 0.0 copy-start.1
  6.5 0.0 copy-start
  6.5 0.0 copy-start.2
  6.5 0.9 fusion.12
  7.4 32.5 %all-gather.3 = bf16[8,2,7168]{2,1,0:T(2,128)(2,1)S(1)} all-gather(bf16[1,2,7168]{2,1,0:T(2,128)(2,1)S(1)} %fusion.12), channel_id=1, replica_groups=mesh['groups'=2,'vocab'=8,'mp'=2] {'vocab'}, dimensions={0}, use_global_device_ids=true | all-gather | bytes 258048 | tf_op jit(solution)/shard_map/all_gather | solution.py:36
  39.9 0.1 reshape.39
  40.0 9.1 %fusion.14 = f32[16,1024]{1,0:T(8,128)S(1)} fusion(bf16[16,7168]{1,0:T(8,128)(2,1)S(1)} %reshape.39, bf16[1024,7168]{1,0:T(8,128)(2,1)} %param.11), kind=kOutput, calls=%fused_computation.28 | convolution fusion | flops 234881024 | bytes 14974976 | tf_op jit(solution)/shard_map/dot_general | solution.py:35
  49.1 0.7 reshape.18
  49.7 5.5 %all-to-all-start = ((f32[8,2,1,1024]{3,1,2,0:T(2,128)}), f32[8,2,1,1024]{3,1,2,0:T(2,128)S(1)}, u32[]{:S(2)}, u32[]{:S(2)}) async-start(f32[8,2,1,1024]{3,1,2,0:T(2,128)} %bitcast.4), calls=%async_computation | async-start | bytes 131072 | tf_op jit(solution)/shard_map/all_to_all | solution.py:45
  55.2 0.0 reduce-scatter.2.cloned.1.call-start
  55.3 0.0 copy-done.1
  55.3 6.8 %all-to-all-done = f32[8,2,1,1024]{3,1,2,0:T(2,128)S(1)} async-done(((f32[8,2,1,1024]{3,1,2,0:T(2,128)}), f32[8,2,1,1024]{3,1,2,0:T(2,128)S(1)}, u32[]{:S(2)}, u32[]{:S(2)}) %all-to-all-start) | async-done | bytes 65568 | tf_op jit(solution)/shard_map/all_to_all | solution.py:45
  62.2 0.1 copy.10
  62.2 3.8 %all_to_all.27 = f32[1,2,1,8192]{3,2,0,1:T(1,128)S(1)} all-to-all(f32[1,2,1,8192]{3,2,0,1:T(1,128)S(1)} %copy.10), channel_id=1, replica_groups=mesh['groups'=2,'vocab'=8,'mp'=2] {'mp'}, dimensions={1} | all-to-all | bytes 131072 | tf_op jit(solution)/shard_map/all_to_all | solution.py:44
  66.0 0.1 reduce_sum.38
  66.1 0.0 copy-done
  66.2 0.7 multiply_reduce_fusion
  67.5 0.1 convert_bitcast_fusion
  67.6 19.5 %all-gather.4 = bf16[16,1,8192]{2,1,0:T(2,128)(2,1)S(1)} all-gather(bf16[1,1,8192]{2,1,0:T(2,128)(2,1)S(1)} %convert_bitcast_fusion), channel_id=1, replica_groups=mesh['groups'=2,'vocab'=8,'mp'=2] {'vocab','mp'}, dimensions={0}, use_global_device_ids=true | all-gather | bytes 278528 | tf_op jit(solution)/shard_map/all_gather | solution.py:61
  87.0 0.3 constant_dynamic-slice_fusion.3
  87.3 4.0 %fusion.7 = f32[16,504]{1,0:T(8,128)} fusion(bf16[4096,504]{0,1:T(8,128)(2,1)} %param.14, bf16[16,1,4096]{2,1,0:T(2,128)(2,1)S(1)} %constant_dynamic-slice_fusion.3), kind=kOutput, calls=%fused_computation.11 | convolution fusion | flops 66060288 | bytes 4292096 | tf_op jit(solution)/shard_map/dot_general | solution.py:66
  91.3 0.0 reduce-scatter.2.cloned.1.call-update
  91.3 0.0 copy-done.2
  91.4 0.0 copy-done.3
  91.4 0.6 dynamic-slice
  92.7 4.2 %reduce-scatter.2.cloned.1.call-done = f32[8,504]{1,0:T(8,128)} async-done(((f32[16,504]{1,0:T(8,128)}), f32[8,504]{1,0:T(8,128)}) %reduce-scatter.2.cloned.1.call-update) | async-done | bytes 16144 | tf_op jit(solution)/shard_map/reduce_scatter | solution.py:67
  96.8 0.8 reduce_max.9
  97.7 0.2 dynamic-update-slice
  97.9 0.9 select_reduce_fusion
  98.9 0.2 dynamic-update-slice.2
  99.1 0.2 dynamic-update-slice.1
  99.3 21.5 %all-reduce.3 = (f32[64]{0:T(128)S(1)}, f32[64]{0:T(128)S(1)}, f32[64]{0:T(128)S(1)}) all-reduce(f32[64]{0:T(128)S(1)} %dynamic-update-slice, f32[64]{0:T(128)S(1)} %dynamic-update-slice.1, f32[64]{0:T(128)S(1)} %dynamic-update-slice.2), channel_id=2, replica_groups=mesh['groups'=2,'vocab'=8,'mp'=2] {'vocab'}, use_global_device_ids=true, to_apply=%add | all-reduce | flops 192 | bytes 1536
  120.9 0.1 reshape.20
  120.9 0.1 reshape.21
  121.0 0.1 reshape.22
  121.1 0.3 while.19
  121.4 0.5 log_subtract_fusion
  (13 shorter events, 0.3 us)
Async XLA Ops:
  6.5 84.8 %copy-start.3 = (u32[32]{0:T(128)S(1)}, u32[32]{0:T(128)}, u32[]{:S(2)}) copy-start(u32[32]{0:T(128)} %constant.71) | copy-start | bytes 388
  6.5 48.8 %copy-start.1 = (bf16[8192]{0:T(1024)(128)(2,1)S(1)}, bf16[8192]{0:T(1024)(128)(2,1)}, u32[]{:S(2)}) copy-start(bf16[8192]{0:T(1024)(128)(2,1)} %param.13) | copy-start | bytes 49156
  6.5 59.6 %copy-start = (bf16[1,8192]{1,0:T(2,128)(2,1)S(1)}, bf16[1,8192]{1,0:T(2,128)(2,1)}, u32[]{:S(2)}) copy-start(bf16[1,8192]{1,0:T(2,128)(2,1)} %param.12) | copy-start | bytes 49156
  6.5 84.8 %copy-start.2 = (s32[8]{0:T(128)S(1)}, s32[8]{0:T(128)}, u32[]{:S(2)}) copy-start(s32[8]{0:T(128)} %param.15) | copy-start | bytes 100
  49.7 12.4 %all-to-all-start = ((f32[8,2,1,1024]{3,1,2,0:T(2,128)}), f32[8,2,1,1024]{3,1,2,0:T(2,128)S(1)}, u32[]{:S(2)}, u32[]{:S(2)}) async-start(f32[8,2,1,1024]{3,1,2,0:T(2,128)} %bitcast.4), calls=%async_computation | async-start | bytes 131072 | tf_op jit(solution)/shard_map/all_to_all | solution.py:45
  55.2 41.6 %reduce-scatter.2.cloned.1.call-start = ((), (), s32[]{:S(2)}) async-start(), calls=%async_computation.3 | async-start | bytes 49152 | tf_op jit(solution)/shard_map/reduce_scatter | solution.py:67
Sparse Core Ops, SparseCore 0:
  91.4 5.3 reduce-scatter.1
where the time goes:
time: 129 us
  blocking collectives  77.3 us (60%)
  between operations  14.9 us (12%)
  matrix products  13 us (10%)
  waiting for transfers between devices  11 us (9%)
  starting transfers between devices  5.54 us (4%)
  other arithmetic  4.22 us (3%)
  local copies, waits for them, and re-layouts  2.68 us (2%)
    all_gather x1, blocking collectives, body(): lax.all_gather(gated_units, 'vocab', axis=0, tiled=True)  32.5 us
    unnamed x1, blocking collectives  21.5 us
    all_gather x1, blocking collectives, body(): lax.all_gather(normed, ('vocab', 'mp'), axis=0, tiled=True)  19.5 us
    dot_general x1, matrix products, body(): lax.dot_general(lax.all_gather(gated_units, 'vocab', axis=0, tiled=True),...  9.05 us
    all_to_all x1, waiting for transfers between devices, body(): lax.all_to_all(grouped, 'vocab', split_axis=0, concat_axis=3, tiled=True)  6.83 us
    all_to_all x1, starting transfers between devices, body(): lax.all_to_all(grouped, 'vocab', split_axis=0, concat_axis=3, tiled=True)  5.51 us
    reduce_scatter x1, waiting for transfers between devices, body(): lax.psum_scatter(logit_terms, 'mp', scatter_dimension=0, tiled=True)  4.19 us
    dot_general x1, matrix products, body(): jnp.dot(halves, head_weight, preferred_element_type=jnp.float32)  3.98 us
  transfers between devices with their start and end apart: 2, of which 2 were waited for; matrix products, arithmetic and copies ran while one was open for 1% of the time, Pallas kernels for 0%

commit v1 on v0

--- a/solution.py
+++ b/solution.py
@@ -41,13 +41,10 @@
     own_rows = residual.shape[0]
     block_cols = down_weight.shape[0]
     grouped = down_terms.reshape(vocab_count, model_count, own_rows, block_cols)
-    arrived = lax.all_to_all(
-        lax.all_to_all(grouped, "vocab", split_axis=0, concat_axis=3, tiled=True),
-        "mp",
-        split_axis=1,
-        concat_axis=0,
-        tiled=True,
-    )
+    own = lax.all_to_all(grouped, "vocab", split_axis=0, concat_axis=3, tiled=True)
+    parts = jnp.split(own, lax.axis_size("mp"), axis=1)
+    got = lax.all_to_all(jnp.stack(parts), "mp", 0, 0)
+    arrived = jnp.concatenate(got, axis=0)
     update = jnp.sum(arrived, axis=(0, 1))
     stream = (residual.astype(jnp.float32) + update).astype(jnp.bfloat16)
     stream = lax.optimization_barrier(stream)

time: 129 us -> 129 us (level)
  no operation moved by 1% of the time
where the time goes in v1:
time: 129 us
  blocking collectives  77.3 us (60%)
  between operations  14.9 us (12%)
  matrix products  13 us (10%)
  waiting for transfers between devices  11 us (9%)
  starting transfers between devices  5.54 us (4%)
  other arithmetic  4.28 us (3%)
  local copies, waits for them, and re-layouts  2.66 us (2%)
    all_gather x1, blocking collectives, body(): lax.all_gather(gated_units, 'vocab', axis=0, tiled=True)  32.5 us
    unnamed x1, blocking collectives  21.5 us
    all_gather x1, blocking collectives, body(): lax.all_gather(normed, ('vocab', 'mp'), axis=0, tiled=True)  19.5 us
    dot_general x1, matrix products, body(): lax.dot_general(lax.all_gather(gated_units, 'vocab', axis=0, tiled=True),...  9.05 us
    all_to_all x1, waiting for transfers between devices, body(): lax.all_to_all(grouped, 'vocab', split_axis=0, concat_axis=3, tiled=True)  6.83 us
    all_to_all x1, starting transfers between devices, body(): lax.all_to_all(grouped, 'vocab', split_axis=0, concat_axis=3, tiled=True)  5.51 us
    reduce_scatter x1, waiting for transfers between devices, body(): lax.psum_scatter(logit_terms, 'mp', scatter_dimension=0, tiled=True)  4.19 us
    dot_general x1, matrix products, body(): jnp.dot(halves, head_weight, preferred_element_type=jnp.float32)  3.98 us
  transfers between devices with their start and end apart: 2, of which 2 were waited for; matrix products, arithmetic and copies ran while one was open for 1% of the time, Pallas kernels for 0%

profile of v1, /device:TPU:0, one launch (start us, length us, event | category | flops | bytes accessed | tf_op | source)
XLA Modules:
  0.0 128.8 jit_solution(17891329190113405173)
XLA Ops:
  6.5 0.0 copy-start.3
  6.5 0.0 copy-start.1
  6.5 0.0 copy-start
  6.5 0.0 copy-start.2
  6.5 0.9 fusion.12
  7.4 32.5 %all-gather.3 = bf16[8,2,7168]{2,1,0:T(2,128)(2,1)S(1)} all-gather(bf16[1,2,7168]{2,1,0:T(2,128)(2,1)S(1)} %fusion.12), channel_id=1, replica_groups=mesh['groups'=2,'vocab'=8,'mp'=2] {'vocab'}, dimensions={0}, use_global_device_ids=true | all-gather | bytes 258048 | tf_op jit(solution)/shard_map/all_gather | solution.py:36
  39.9 0.1 reshape.38
  40.0 9.1 %fusion.14 = f32[16,1024]{1,0:T(8,128)S(1)} fusion(bf16[16,7168]{1,0:T(8,128)(2,1)S(1)} %reshape.38, bf16[1024,7168]{1,0:T(8,128)(2,1)} %param.11), kind=kOutput, calls=%fused_computation.31 | convolution fusion | flops 234881024 | bytes 14974976 | tf_op jit(solution)/shard_map/dot_general | solution.py:35
  49.1 0.7 reshape.17
  49.7 5.5 %all-to-all-start = ((f32[8,2,1,1024]{3,1,2,0:T(2,128)}), f32[8,2,1,1024]{3,1,2,0:T(2,128)S(1)}, u32[]{:S(2)}, u32[]{:S(2)}) async-start(f32[8,2,1,1024]{3,1,2,0:T(2,128)} %bitcast.4), calls=%async_computation | async-start | bytes 131072 | tf_op jit(solution)/shard_map/all_to_all | solution.py:44
  55.2 0.0 reduce-scatter.2.cloned.1.call-start
  55.3 0.0 copy-done.1
  55.3 6.8 %all-to-all-done = f32[8,2,1,1024]{3,1,2,0:T(2,128)S(1)} async-done(((f32[8,2,1,1024]{3,1,2,0:T(2,128)}), f32[8,2,1,1024]{3,1,2,0:T(2,128)S(1)}, u32[]{:S(2)}, u32[]{:S(2)}) %all-to-all-start) | async-done | bytes 65568 | tf_op jit(solution)/shard_map/all_to_all | solution.py:44
  62.2 0.1 slice_bitcast_fusion.1
  62.2 0.1 pad_maximum_fusion
  62.3 3.8 %all_to_all.23 = f32[2,1,1,1,8192]{4,3,2,1,0:T(1,128)S(1)} all-to-all(f32[2,1,1,1,8192]{4,3,2,1,0:T(1,128)S(1)} %pad_maximum_fusion), channel_id=1, replica_groups=mesh['groups'=2,'vocab'=8,'mp'=2] {'mp'}, dimensions={0} | all-to-all | bytes 131072 | tf_op jit(solution)/shard_map/all_to_all | solution.py:46
  66.1 0.1 reduce_sum.38
  66.2 0.0 copy-done
  66.2 0.7 multiply_reduce_fusion
  67.6 0.1 convert_bitcast_fusion
  67.6 19.5 %all-gather.4 = bf16[16,1,8192]{2,1,0:T(2,128)(2,1)S(1)} all-gather(bf16[1,1,8192]{2,1,0:T(2,128)(2,1)S(1)} %convert_bitcast_fusion), channel_id=1, replica_groups=mesh['groups'=2,'vocab'=8,'mp'=2] {'vocab','mp'}, dimensions={0}, use_global_device_ids=true | all-gather | bytes 278528 | tf_op jit(solution)/shard_map/all_gather | solution.py:58
  87.1 0.3 constant_dynamic-slice_fusion.3
  87.4 4.0 %fusion.7 = f32[16,504]{1,0:T(8,128)} fusion(bf16[4096,504]{0,1:T(8,128)(2,1)} %param.14, bf16[16,1,4096]{2,1,0:T(2,128)(2,1)S(1)} %constant_dynamic-slice_fusion.3), kind=kOutput, calls=%fused_computation.11 | convolution fusion | flops 66060288 | bytes 4292096 | tf_op jit(solution)/shard_map/dot_general | solution.py:63
  91.4 0.0 reduce-scatter.2.cloned.1.call-update
  91.4 0.0 copy-done.2
  91.4 0.0 copy-done.3
  91.4 0.6 dynamic-slice
  92.7 4.2 %reduce-scatter.2.cloned.1.call-done = f32[8,504]{1,0:T(8,128)} async-done(((f32[16,504]{1,0:T(8,128)}), f32[8,504]{1,0:T(8,128)}) %reduce-scatter.2.cloned.1.call-update) | async-done | bytes 16144 | tf_op jit(solution)/shard_map/reduce_scatter | solution.py:64
  96.9 0.8 reduce_max.9
  97.7 0.2 dynamic-update-slice
  98.0 0.9 select_reduce_fusion
  98.9 0.2 dynamic-update-slice.2
  99.2 0.2 dynamic-update-slice.1
  99.4 21.5 %all-reduce.3 = (f32[64]{0:T(128)S(1)}, f32[64]{0:T(128)S(1)}, f32[64]{0:T(128)S(1)}) all-reduce(f32[64]{0:T(128)S(1)} %dynamic-update-slice, f32[64]{0:T(128)S(1)} %dynamic-update-slice.1, f32[64]{0:T(128)S(1)} %dynamic-update-slice.2), channel_id=2, replica_groups=mesh['groups'=2,'vocab'=8,'mp'=2] {'vocab'}, use_global_device_ids=true, to_apply=%add | all-reduce | flops 192 | bytes 1536
  120.9 0.1 reshape.19
  121.0 0.1 reshape.20
  121.1 0.1 reshape.21
  121.1 0.3 while.19
  121.4 0.5 log_subtract_fusion
  (13 shorter events, 0.3 us)
Async XLA Ops:
  6.5 84.9 %copy-start.3 = (u32[32]{0:T(128)S(1)}, u32[32]{0:T(128)}, u32[]{:S(2)}) copy-start(u32[32]{0:T(128)} %constant.71) | copy-start | bytes 388
  6.5 48.8 %copy-start.1 = (bf16[8192]{0:T(1024)(128)(2,1)S(1)}, bf16[8192]{0:T(1024)(128)(2,1)}, u32[]{:S(2)}) copy-start(bf16[8192]{0:T(1024)(128)(2,1)} %param.13) | copy-start | bytes 49156
  6.5 59.6 %copy-start = (bf16[1,8192]{1,0:T(2,128)(2,1)S(1)}, bf16[1,8192]{1,0:T(2,128)(2,1)}, u32[]{:S(2)}) copy-start(bf16[1,8192]{1,0:T(2,128)(2,1)} %param.12) | copy-start | bytes 49156
  6.5 84.8 %copy-start.2 = (s32[8]{0:T(128)S(1)}, s32[8]{0:T(128)}, u32[]{:S(2)}) copy-start(s32[8]{0:T(128)} %param.15) | copy-start | bytes 100
  49.7 12.4 %all-to-all-start = ((f32[8,2,1,1024]{3,1,2,0:T(2,128)}), f32[8,2,1,1024]{3,1,2,0:T(2,128)S(1)}, u32[]{:S(2)}, u32[]{:S(2)}) async-start(f32[8,2,1,1024]{3,1,2,0:T(2,128)} %bitcast.4), calls=%async_computation | async-start | bytes 131072 | tf_op jit(solution)/shard_map/all_to_all | solution.py:44
  55.2 41.7 %reduce-scatter.2.cloned.1.call-start = ((), (), s32[]{:S(2)}) async-start(), calls=%async_computation.3 | async-start | bytes 49152 | tf_op jit(solution)/shard_map/reduce_scatter | solution.py:64
Sparse Core Ops, SparseCore 0:
  91.5 5.3 reduce-scatter.1
